TPU v7x, 512 devices: a whole 4x4x16 slice. The times are simulated.
512 devices in a mesh: gx: 16 (over x, y_lo, core), gy: 32 (over y_hi, z).
Axes of the slice: x: 4, y: 4 (y_hi: 2, y_lo: 2; y = y_hi * 2 + y_lo), z: 16, core: 2. Of those that a mesh axis runs over, the one named last changes fastest.
Arguments:
- plate_motion: bfloat16 [32, 64, 128, 2, 128], P('gx', 'gy'), may hold values from -6 to 6
- adjoint_load: bfloat16 [32, 64, 128, 2, 128], P('gx', 'gy'), may hold values from -6 to 6
- excitation: bfloat16 [32, 64, 128, 2, 128], P('gx', 'gy'), may hold values from -6 to 6
- coupling: bfloat16 [32, 64, 5, 2, 128, 128], P('gx', 'gy'), may hold values from -0.25 to 0.25
- joints: int32 [32, 64, 4], P('gx', 'gy'), may hold values 0 or 1
- hydro: bfloat16 [2, 16384, 16384], P(None, 'gx', 'gy'), may hold values from -0.046875 to 0.046875
- panel_map: bfloat16 [16384, 2, 2, 128], P(('gx', 'gy')), may hold values from -0.25 to 0.25
Outputs:
- residual: float32 [32, 64, 128, 2, 128], P('gx', 'gy')
- multiplier: float32 [32, 64, 128, 2, 128], P('gx', 'gy')
- sensitivity: float32 [32, 64], P('gx', 'gy')
All inputs are finite; a program needn't handle non-finite values. No bound on the sum of `joints` on one device may be relied on, other than what follows from the above.
Results may differ from a plain program's by a relative error of at most 0.0031.
Values may be sent and summed in bfloat16 or wider, within the bound.
A program may use at most 64 MiB of HBM per device.

v0:
```python
import math
import jax
import jax.numpy as jnp
from jax import lax
from jax.sharding import PartitionSpec as P


def extended(x, sides, width):
    for axis, dim in sides:
        size, length = (lax.axis_size(axis), x.shape[dim])
        up = [(i, (i + 1) % size) for i in range(size - 1)]
        down = [(j, i) for i, j in up]
        last = lax.slice_in_dim(x, length - width, length, axis=dim)
        first = lax.slice_in_dim(x, 0, width, axis=dim)
        before = lax.ppermute(last, axis, up)
        after = lax.ppermute(first, axis, down)
        x = jnp.concatenate([before, x, after], axis=dim)
    return x


def complex_apply(form, coupling, vector):
    real_c = coupling[..., 0, :, :]
    imag_c = coupling[..., 1, :, :]
    real_v = vector[..., 0, :]
    imag_v = vector[..., 1, :]

    def mult(matrix, values):
        return jnp.einsum(form, matrix, values, preferred_element_type=jnp.float32)

    return jnp.stack(
        [mult(real_c, real_v) - mult(imag_c, imag_v), mult(real_c, imag_v) + mult(imag_c, real_v)],
        axis=-2,
    )


def adjoint_apply(form, coupling, vector):
    real_c = coupling[..., 0, :, :]
    imag_c = coupling[..., 1, :, :]
    real_v = vector[..., 0, :]
    imag_v = vector[..., 1, :]

    def mult(matrix, values):
        return jnp.einsum(form, matrix, values, preferred_element_type=jnp.float32)

    return jnp.stack(
        [mult(real_c, real_v) + mult(imag_c, imag_v), mult(real_c, imag_v) - mult(imag_c, real_v)],
        axis=-2,
    )


def plain_product(matrix, values):
    return jnp.dot(matrix, values, preferred_element_type=jnp.float32)


def flipped_product(matrix, values):
    return lax.dot_general(
        matrix, values, (((0,), (0,)), ((), ())), preferred_element_type=jnp.float32
    )


def on_device(plate_motion, adjoint_load, excitation, coupling, joints, hydro, panel_map):
    rows_count = plate_motion.shape[0]
    cols_count = plate_motion.shape[1]
    panel_count = panel_map.shape[0]
    unknowns = plate_motion.shape[4]
    cases = plate_motion.shape[2]
    links = joints.astype(jnp.float32)[:, :, :, None, None, None]
    padded = extended(plate_motion, (("gx", 0), ("gy", 1)), 1)
    beside_all = jnp.stack(
        [
            padded[0:rows_count, 1:-1],
            padded[2:, 1:-1],
            padded[1:-1, 0:cols_count],
            padded[1:-1, 2:],
        ],
        axis=2,
    )
    own = complex_apply("xyij,xyhj->xyhi", coupling[:, :, 0], plate_motion)
    structural = own + jnp.sum(
        links * complex_apply("xydij,xydhj->xydhi", coupling[:, :, 1:], beside_all), axis=2
    )
    outgoing = links * adjoint_apply("xydji,xyhj->xydhi", coupling[:, :, 1:], adjoint_load)
    own_adjoint = adjoint_apply("xyji,xyhj->xyhi", coupling[:, :, 0], adjoint_load)
    layered = extended(outgoing, (("gx", 0), ("gy", 1)), 1)
    incoming = (
        layered[2:, 1:-1, 0] + layered[:-2, 1:-1, 1] + layered[1:-1, 2:, 2] + layered[1:-1, :-2, 3]
    )
    lift = math.sqrt(rows_count * cols_count * unknowns / panel_count)
    motion_panels = jnp.einsum(
        "nxyk,xyhck->cnh", panel_map, plate_motion, preferred_element_type=jnp.float32
    ).astype(jnp.bfloat16)
    load_panels = jnp.einsum(
        "nxyk,xyhck->cnh", panel_map, adjoint_load, preferred_element_type=jnp.float32
    ).astype(jnp.bfloat16)
    piece = lax.all_gather(motion_panels, "gx", axis=1, tiled=True)
    first = plain_product(hydro[0], piece[0]) - plain_product(hydro[1], piece[1])
    second = plain_product(hydro[0], piece[1]) + plain_product(hydro[1], piece[0])
    pressure_part = jnp.stack([first, second])
    piece = lax.all_gather(load_panels, "gy", axis=1, tiled=True)
    first = flipped_product(hydro[0], piece[0]) + flipped_product(hydro[1], piece[1])
    second = flipped_product(hydro[0], piece[1]) - flipped_product(hydro[1], piece[0])
    reaction_part = jnp.stack([first, second])
    pressure_band = lax.psum(pressure_part, "gy")
    pressure = lax.dynamic_slice_in_dim(
        pressure_band, lax.axis_index("gy") * panel_count, panel_count, 1
    )
    reaction_band = lax.psum(reaction_part, "gx")
    reaction = lax.dynamic_slice_in_dim(
        reaction_band, lax.axis_index("gx") * panel_count, panel_count, 1
    )
    pressure = pressure.astype(jnp.bfloat16)
    reaction = reaction.astype(jnp.bfloat16)
    pressure_force = jnp.einsum(
        "nxyk,cnh->xyhck", panel_map, pressure, preferred_element_type=jnp.float32
    )
    reaction_force = jnp.einsum(
        "nxyk,cnh->xyhck", panel_map, reaction, preferred_element_type=jnp.float32
    )
    residual = structural + lift * pressure_force - excitation.astype(jnp.float32)
    multiplier = own_adjoint + incoming + lift * reaction_force
    sensitivity = jnp.sum(multiplier * own, axis=(2, 3, 4)) / math.sqrt(cases * unknowns)
    return (residual, multiplier, sensitivity)


def solution(mesh):
    placed = (
        P("gx", "gy", None, None, None),
        P("gx", "gy", None, None, None),
        P("gx", "gy", None, None, None),
        P("gx", "gy", None, None, None, None),
        P("gx", "gy", None),
        P(None, "gx", "gy"),
        P(("gx", "gy"), None, None, None),
    )
    return jax.shard_map(
        on_device,
        mesh=mesh,
        in_specs=placed,
        out_specs=(P("gx", "gy", None, None, None), P("gx", "gy", None, None, None), P("gx", "gy")),
        check_vma=False,
    )
```

profile of v0, /device:TPU:14, one launch (start us, length us, event | category | flops | bytes accessed | tf_op | source)
XLA Modules:
  0.0 440.0 jit_solution(6919222201309677431)
XLA Ops:
  0.6 1.0 copy.43
  1.7 0.7 fusion.106
  2.4 1.9 collective-permute-start
  4.3 3.6 collective-permute-start.1
  8.0 1.3 slice_bitcast_fusion.2
  9.4 1.3 fusion.59
  10.6 0.3 fusion.57
  10.9 1.0 copy_bitcast_fusion
  11.9 0.2 fusion.19
  12.1 84.5 %all_gather.7 = bf16[2,1024,128]{2,1,0:T(8,128)(2,1)S(1)} all-gather(bf16[2,32,128]{2,1,0:T(8,128)(2,1)S(1)} %fusion.19), channel_id=1, replica_groups=mesh['gx'=16,'gy'=32] {'gy'}, dimensions={1}, use_global_device_ids=true | all-gather | bytes 540672 | tf_op jit(solution)/shard_map/all_gather | solution.py:99
  96.6 1.2 fusion.25
  97.9 1.2 fusion.27
  99.1 0.2 fusion.20
  99.3 16.8 %all_gather.6 = bf16[2,512,128]{2,1,0:T(8,128)(2,1)S(1)} all-gather(bf16[2,32,128]{2,1,0:T(8,128)(2,1)S(1)} %fusion.20), channel_id=1, replica_groups=mesh['gx'=16,'gy'=32] {'gx'}, dimensions={1}, use_global_device_ids=true | all-gather | bytes 278528 | tf_op jit(solution)/shard_map/all_gather | solution.py:95
  116.2 1.2 fusion.29
  117.4 1.2 fusion.31
  118.6 0.1 copy.46
  118.7 0.2 fusion.71
  118.9 2.0 fusion.15
  120.9 1.6 fusion.16
  122.6 0.4 fusion.5
  123.0 0.4 fusion.6
  123.5 0.3 copy-done
  123.8 0.3 fusion.2
  124.1 0.3 fusion.1
  124.4 0.6 copy-done.5
  125.0 0.1 constant_dynamic-update-slice_fusion.1
  125.1 0.9 constant_dynamic-update-slice_fusion
  126.1 1.3 collective-permute-start.2
  127.4 1.3 collective-permute-start.3
  128.7 1.1 pad_maximum_fusion.2
  129.9 0.9 fusion.66
  130.8 2.9 collective-permute-done.2
  133.7 4.1 collective-permute-done.3
  137.9 0.1 pad_maximum_fusion.1
  138.1 0.1 slice_bitcast_fusion.1
  138.1 0.5 fusion.51
  138.6 0.5 fusion.47
  139.1 0.5 fusion.4
  139.6 0.5 fusion.3
  140.1 1.3 maximum_multiply_fusion.1
  141.3 1.6 fusion.104
  142.9 1.9 collective-permute-start.4
  144.8 3.4 collective-permute-start.5
  148.2 0.8 pad_maximum_fusion.12
  149.0 0.2 fusion.11
  149.2 0.2 fusion.75
  149.4 0.9 fusion.12
  150.3 0.2 fusion.78
  150.5 0.2 fusion.77
  150.7 18.0 %collective-permute-done.4 = f32[1,2,4,128,2,128]{5,3,1,0,4,2:T(8,128)} collective-permute-done((f32[1,2,4,128,2,128]{5,3,1,0,4,2:T(8,128)}, f32[1,2,4,128,2,128]{5,3,1,0,4,2:T(8,128)}, u32[]{:S(2)}, u32[]{:S(2)}) %collective-permute-start.4) | collective-permute-done | bytes 1048608 | tf_op jit(solution)/shard_map/ppermute | solution.py:16
  168.7 2.0 pad_maximum_fusion
  170.7 2.5 fusion.103
  173.2 1.4 collective-permute-start.6
  174.6 5.9 %collective-permute-start.7 = (f32[4,1,4,128,2,128]{5,3,1,0,4,2:T(8,128)}, f32[4,1,4,128,2,128]{5,3,1,0,4,2:T(8,128)}, u32[]{:S(2)}, u32[]{:S(2)}) collective-permute-start(f32[4,1,4,128,2,128]{5,3,1,0,4,2:T(8,128)} %get-tuple-element.10), channel_id=1, source_target_pairs={{0,1},{1,2},{2,3},{3,4},{4,5},{5,6},{6,7},{7,8},{8,9},{9,10},{10,1... | collective-permute-start | bytes 6291464 | tf_op jit(solution)/shard_map/ppermute | solution.py:15
  180.5 0.2 fusion.13
  180.7 0.2 fusion.14
  181.0 98.1 %all-reduce.2 = bf16[2,512,128]{2,1,0:T(8,128)(2,1)} all-reduce(f32[2,512,128]{2,1,0:T(8,128)} %pad_maximum_fusion.12), channel_id=1, replica_groups=mesh['gx'=16,'gy'=32] {'gx'}, use_global_device_ids=true, to_apply=%region_2.0 | all-reduce | flops 131072 | bytes 786432 | tf_op jit(solution)/shard_map/psum | solution.py:107
  279.1 154.9 %all-reduce.3 = bf16[2,1024,128]{2,1,0:T(8,128)(2,1)} all-reduce(f32[2,1024,128]{2,1,0:T(8,128)} %pad_maximum_fusion.2), channel_id=1, replica_groups=mesh['gx'=16,'gy'=32] {'gy'}, use_global_device_ids=true, to_apply=%region_1.0 | all-reduce | flops 262144 | bytes 1572864 | tf_op jit(solution)/shard_map/psum | solution.py:103
  434.0 1.4 fusion.10
  435.4 1.2 copy.80
  436.6 1.6 multiply_reduce_fusion
  438.2 1.2 copy.81
  439.4 0.6 broadcast_multiply_fusion
  (34 shorter events, 0.2 us)
Async XLA Ops:
  0.6 8.6 %copy-start.9 = (bf16[2,2,128,2,128]{4,3,2,1,0:T(2,128)(2,1)S(1)}, bf16[2,2,128,2,128]{4,3,2,1,0:T(2,128)(2,1)}, u32[]{:S(2)}) copy-start(bf16[2,2,128,2,128]{4,3,2,1,0:T(2,128)(2,1)} %param.8) | copy-start | bytes 786436
  2.4 122.0 %collective-permute-start = (bf16[1,2,128,2,128]{4,2,1,0,3:T(8,128)(2,1)}, bf16[1,2,128,2,128]{4,2,1,0,3:T(8,128)(2,1)S(1)}, u32[]{:S(2)}, u32[]{:S(2)}) collective-permute-start(bf16[1,2,128,2,128]{4,2,1,0,3:T(8,128)(2,1)} %get-tuple-element.24), channel_id=1, source_target_pairs={{0,32},{32,64},{64,96},{96,128},{128,160},{160,192},{192,224},{224... | collective-permute-start | bytes 393224 | tf_op jit(solution)/shard_map/ppermute | solution.py:15
  4.3 120.8 %collective-permute-start.1 = (bf16[1,2,128,2,128]{4,2,1,0,3:T(8,128)(2,1)}, bf16[1,2,128,2,128]{4,2,1,0,3:T(8,128)(2,1)}, u32[]{:S(2)}, u32[]{:S(2)}) collective-permute-start(bf16[1,2,128,2,128]{4,2,1,0,3:T(8,128)(2,1)} %get-tuple-element.23), channel_id=1, source_target_pairs={{32,0},{64,32},{96,64},{128,96},{160,128},{192,160},{224,192},{256... | collective-permute-start | bytes 393224 | tf_op jit(solution)/shard_map/ppermute | solution.py:16
  9.3 2.6 copy-start.10
  9.3 87.3 %copy-start.1 = (bf16[2,1024,512]{2,1,0:T(8,128)(2,1)S(1)}, bf16[2,1024,512]{2,1,0:T(8,128)(2,1)}, u32[]{:S(2)}) copy-start(bf16[2,1024,512]{2,1,0:T(8,128)(2,1)} %param.12) | copy-start | bytes 6291460
  12.1 87.0 %copy-start.4 = (bf16[2,2,128,2,128]{4,3,2,1,0:T(2,128)(2,1)S(1)}, bf16[2,2,128,2,128]{4,3,2,1,0:T(2,128)(2,1)}, u32[]{:S(2)}) copy-start(bf16[2,2,128,2,128]{4,3,2,1,0:T(2,128)(2,1)} %param.7) | copy-start | bytes 786436
  96.6 19.5 %copy-start.8 = (bf16[2,1024,128]{2,1,0:T(8,128)(2,1)}, bf16[2,1024,128]{2,1,0:T(8,128)(2,1)S(1)}, u32[]{:S(2)}) copy-start(bf16[2,1024,128]{2,1,0:T(8,128)(2,1)S(1)} %all_gather.7) | copy-start | bytes 1572868
  99.1 19.5 %copy-start.12 = (s32[2,2,4]{2,1,0:T(2,128)S(1)}, s32[2,2,4]{2,1,0:T(2,128)}, u32[]{:S(2)}) copy-start(s32[2,2,4]{2,1,0:T(2,128)} %param.11) | copy-start | bytes 196
  118.7 2.2 copy-start.2
  118.7 3.8 copy-start.7
  120.9 2.1 copy-start.6
  122.6 1.2 copy-start
  124.1 1.0 copy-start.5
  126.1 7.6 %collective-permute-start.2 = (bf16[4,1,128,2,128]{4,2,1,0,3:T(8,128)(2,1)S(1)}, bf16[4,1,128,2,128]{4,2,1,0,3:T(8,128)(2,1)S(1)}, u32[]{:S(2)}, u32[]{:S(2)}) collective-permute-start(bf16[4,1,128,2,128]{4,2,1,0,3:T(8,128)(2,1)S(1)} %get-tuple-element.19), channel_id=1, source_target_pairs={{0,1},{1,2},{2,3},{3,4},{4,5},{5,6},{6,7},{7,8},{8,9},{9,10},{10,1... | collective-permute-start | bytes 786440 | tf_op jit(solution)/shard_map/ppermute | solution.py:15
  127.4 10.4 %collective-permute-start.3 = (bf16[4,1,128,2,128]{4,2,1,0,3:T(8,128)(2,1)S(1)}, bf16[4,1,128,2,128]{4,2,1,0,3:T(8,128)(2,1)S(1)}, u32[]{:S(2)}, u32[]{:S(2)}) collective-permute-start(bf16[4,1,128,2,128]{4,2,1,0,3:T(8,128)(2,1)S(1)} %get-tuple-element.20), channel_id=1, source_target_pairs={{1,0},{2,1},{3,2},{4,3},{5,4},{6,5},{7,6},{8,7},{9,8},{10,9},{11,1... | collective-permute-start | bytes 786440 | tf_op jit(solution)/shard_map/ppermute | solution.py:16
  142.9 25.8 %collective-permute-start.4 = (f32[1,2,4,128,2,128]{5,3,1,0,4,2:T(8,128)}, f32[1,2,4,128,2,128]{5,3,1,0,4,2:T(8,128)}, u32[]{:S(2)}, u32[]{:S(2)}) collective-permute-start(f32[1,2,4,128,2,128]{5,3,1,0,4,2:T(8,128)} %get-tuple-element.12), channel_id=1, source_target_pairs={{32,0},{64,32},{96,64},{128,96},{160,128},{192,160},{224,192},{256... | collective-permute-start | bytes 3145736 | tf_op jit(solution)/shard_map/ppermute | solution.py:16
  144.8 23.8 %collective-permute-start.5 = (f32[1,2,4,128,2,128]{5,3,1,0,4,2:T(8,128)}, f32[1,2,4,128,2,128]{5,3,1,0,4,2:T(8,128)}, u32[]{:S(2)}, u32[]{:S(2)}) collective-permute-start(f32[1,2,4,128,2,128]{5,3,1,0,4,2:T(8,128)} %get-tuple-element.11), channel_id=1, source_target_pairs={{0,32},{32,64},{64,96},{96,128},{128,160},{160,192},{192,224},{224... | collective-permute-start | bytes 3145736 | tf_op jit(solution)/shard_map/ppermute | solution.py:15
  173.2 260.8 %copy-start.11 = (bf16[32,2,2,128]{3,2,1,0:T(2,128)(2,1)S(1)}, bf16[32,2,2,128]{3,2,1,0:T(2,128)(2,1)}, u32[]{:S(2)}) copy-start(bf16[32,2,2,128]{3,2,1,0:T(2,128)(2,1)} %param.13) | copy-start | bytes 98308
  173.2 263.4 %collective-permute-start.6 = (f32[4,1,4,128,2,128]{5,3,1,0,4,2:T(8,128)}, f32[4,1,4,128,2,128]{5,3,1,0,4,2:T(8,128)}, u32[]{:S(2)}, u32[]{:S(2)}) collective-permute-start(f32[4,1,4,128,2,128]{5,3,1,0,4,2:T(8,128)} %get-tuple-element.9), channel_id=1, source_target_pairs={{1,0},{2,1},{3,2},{4,3},{5,4},{6,5},{7,6},{8,7},{9,8},{10,9},{11,1... | collective-permute-start | bytes 6291464 | tf_op jit(solution)/shard_map/ppermute | solution.py:16
  174.6 262.0 %collective-permute-start.7 = (f32[4,1,4,128,2,128]{5,3,1,0,4,2:T(8,128)}, f32[4,1,4,128,2,128]{5,3,1,0,4,2:T(8,128)}, u32[]{:S(2)}, u32[]{:S(2)}) collective-permute-start(f32[4,1,4,128,2,128]{5,3,1,0,4,2:T(8,128)} %get-tuple-element.10), channel_id=1, source_target_pairs={{0,1},{1,2},{2,3},{3,4},{4,5},{5,6},{6,7},{7,8},{8,9},{9,10},{10,1... | collective-permute-start | bytes 6291464 | tf_op jit(solution)/shard_map/ppermute | solution.py:15
  434.0 2.7 copy-start.3
where the time goes:
time: 441 us; the launch traced here: 440 us
  blocking collectives  354 us (80%)
  waiting for transfers between devices  25.1 us (6%)
  starting transfers between devices  20.7 us (5%)
  matrix products  19 us (4%)
  local copies, waits for them, and re-layouts  12.8 us (3%)
  other arithmetic  6.95 us (2%)
    psum x1, blocking collectives, on_device(): pressure_band = lax.psum(pressure_part, 'gy')  155 us
    psum x1, blocking collectives, on_device(): reaction_band = lax.psum(reaction_part, 'gx')  98.1 us
    all_gather x1, blocking collectives, on_device(): piece = lax.all_gather(load_panels, 'gy', axis=1, tiled=True)  84.5 us
    ppermute x4, waiting for transfers between devices, extended(): after = lax.ppermute(first, axis, down)  22.1 us
    all_gather x1, blocking collectives, on_device(): piece = lax.all_gather(motion_panels, 'gx', axis=1, tiled=True)  16.8 us
    ppermute x4, starting transfers between devices, extended(): before = lax.ppermute(last, axis, up)  12.5 us
  transfers between devices with their start and end apart: 8, of which 3 were waited for; matrix products, arithmetic and copies ran while one was open for 5% of the time, Pallas kernels for 0%

commit v1 on v0

--- a/solution.py
+++ b/solution.py
@@ -104,7 +104,7 @@
     pressure = lax.dynamic_slice_in_dim(
         pressure_band, lax.axis_index("gy") * panel_count, panel_count, 1
     )
-    reaction_band = lax.psum(reaction_part, "gx")
+    reaction_band = jnp.sum(lax.all_gather(reaction_part, "gx"), 0)
     reaction = lax.dynamic_slice_in_dim(
         reaction_band, lax.axis_index("gx") * panel_count, panel_count, 1
     )

time: 441 us -> 427 us (0.968)
  the two profiles are of different devices: /device:TPU:14 before, /device:TPU:8 now
where the time goes in v1:
time: 427 us
  blocking collectives  276 us (65%)
  waiting for transfers between devices  83.9 us (20%)
  starting transfers between devices  20.1 us (5%)
  between operations  14.5 us (3%)
  matrix products  14 us (3%)
  local copies, waits for them, and re-layouts  10.1 us (2%)
  other arithmetic  8.06 us (2%)
    psum x1, blocking collectives, on_device(): pressure_band = lax.psum(pressure_part, 'gy')  173 us
    all_gather x1, blocking collectives, on_device(): piece = lax.all_gather(load_panels, 'gy', axis=1, tiled=True)  84.4 us
    ppermute x4, waiting for transfers between devices, extended(): before = lax.ppermute(last, axis, up)  79.8 us
    all_gather x1, blocking collectives, on_device(): piece = lax.all_gather(motion_panels, 'gx', axis=1, tiled=True)  18.7 us
    ppermute x4, starting transfers between devices, extended(): before = lax.ppermute(last, axis, up)  11.7 us
  transfers between devices with their start and end apart: 9, of which 3 were waited for; matrix products, arithmetic and copies ran while one was open for 5% of the time, Pallas kernels for 0%

profile of v1, /device:TPU:8, one launch (start us, length us, event | category | flops | bytes accessed | tf_op | source)
XLA Modules:
  0.0 426.9 jit_solution(14185194893389493817)
XLA Ops:
  7.2 0.0 all-gather.3.cloned.1.call-start
  7.2 1.3 fusion.19
  8.5 84.4 %all_gather.13 = bf16[2,1024,128]{2,1,0:T(8,128)(2,1)S(1)} all-gather(bf16[2,32,128]{2,1,0:T(8,128)(2,1)S(1)} %fusion.19), channel_id=1, replica_groups=mesh['gx'=16,'gy'=32] {'gy'}, dimensions={1}, use_global_device_ids=true | all-gather | bytes 540672 | tf_op jit(solution)/shard_map/all_gather | solution.py:99
  92.9 1.5 fusion.25
  94.5 0.3 fusion.27
  94.8 0.3 fusion.15
  95.2 0.3 fusion.16
  95.6 1.0 copy.109
  96.7 0.7 fusion.106
  97.4 1.9 collective-permute-start.1
  99.3 2.4 collective-permute-start
  101.7 1.0 copy.101
  102.7 0.1 copy.80
  102.8 0.2 fusion.20
  103.0 18.7 %all_gather.12 = bf16[2,512,128]{2,1,0:T(8,128)(2,1)S(1)} all-gather(bf16[2,32,128]{2,1,0:T(8,128)(2,1)S(1)} %fusion.20), channel_id=1, replica_groups=mesh['gx'=16,'gy'=32] {'gx'}, dimensions={1}, use_global_device_ids=true | all-gather | bytes 278528 | tf_op jit(solution)/shard_map/all_gather | solution.py:95
  121.7 1.0 copy_bitcast_fusion
  122.6 0.2 fusion.78
  122.9 0.1 slice_bitcast_fusion.2
  123.0 0.3 fusion.59
  123.3 0.3 fusion.57
  123.5 0.4 fusion.29
  124.0 0.3 fusion.2
  124.3 0.1 constant_dynamic-update-slice_fusion.1
  124.5 1.3 collective-permute-start.2
  125.8 1.3 collective-permute-start.3
  127.1 0.3 fusion.1
  127.4 4.7 %collective-permute-done.2 = bf16[4,1,128,2,128]{4,2,1,0,3:T(8,128)(2,1)S(1)} collective-permute-done((bf16[4,1,128,2,128]{4,2,1,0,3:T(8,128)(2,1)S(1)}, bf16[4,1,128,2,128]{4,2,1,0,3:T(8,128)(2,1)S(1)}, u32[]{:S(2)}, u32[]{:S(2)}) %collective-permute-start.2) | collective-permute-done | bytes 262176 | tf_op jit(solution)/shard_map/ppermute | solution.py:15
  132.1 4.1 collective-permute-done.3
  136.2 0.1 fusion.64
  136.3 0.1 pad_maximum_fusion.1
  136.4 0.1 slice_bitcast_fusion.1
  136.5 0.5 fusion.47
  137.0 0.5 fusion.3
  137.5 0.5 fusion.51
  138.0 0.5 fusion.4
  138.5 1.3 maximum_multiply_fusion.1
  139.8 0.1 fusion.104
  139.9 2.1 collective-permute-start.5
  142.0 3.9 collective-permute-start.4
  145.9 0.2 fusion.13
  146.1 0.4 fusion.5
  146.6 0.4 fusion.31
  147.0 0.4 fusion.6
  147.4 1.0 pad_maximum_fusion.2
  148.5 0.2 fusion.77
  148.7 75.1 %collective-permute-done.5 = f32[1,2,4,128,2,128]{5,3,1,0,4,2:T(8,128)S(1)} collective-permute-done((f32[1,2,4,128,2,128]{5,3,1,0,4,2:T(8,128)S(1)}, f32[1,2,4,128,2,128]{5,3,1,0,4,2:T(8,128)S(1)}, u32[]{:S(2)}, u32[]{:S(2)}) %collective-permute-start.5) | collective-permute-done | bytes 1048608 | tf_op jit(solution)/shard_map/ppermute | solution.py:15
  223.7 0.4 pad_maximum_fusion
  224.1 0.6 copy-done.2
  224.7 0.3 copy-done.3
  225.1 2.4 fusion.103
  227.5 1.3 collective-permute-start.6
  228.8 5.9 %collective-permute-start.7 = (f32[4,1,4,128,2,128]{5,3,1,0,4,2:T(8,128)}, f32[4,1,4,128,2,128]{5,3,1,0,4,2:T(8,128)}, u32[]{:S(2)}, u32[]{:S(2)}) collective-permute-start(f32[4,1,4,128,2,128]{5,3,1,0,4,2:T(8,128)} %get-tuple-element.13), channel_id=1, source_target_pairs={{0,1},{1,2},{2,3},{3,4},{4,5},{5,6},{6,7},{7,8},{8,9},{9,10},{10,1... | collective-permute-start | bytes 6291464 | tf_op jit(solution)/shard_map/ppermute | solution.py:15
  234.7 0.2 fusion.14
  234.9 0.2 fusion.75
  235.1 0.2 fusion.12
  235.3 0.2 fusion.71
  235.5 0.9 fusion.11
  236.3 173.1 %all-reduce.1 = bf16[2,1024,128]{2,1,0:T(8,128)(2,1)} all-reduce(f32[2,1024,128]{2,1,0:T(8,128)} %pad_maximum_fusion.2), channel_id=1, replica_groups=mesh['gx'=16,'gy'=32] {'gy'}, use_global_device_ids=true, to_apply=%region_1.0 | all-reduce | flops 262144 | bytes 1572864 | tf_op jit(solution)/shard_map/psum | solution.py:103
  409.4 1.4 fusion.10
  410.8 1.2 copy.113
  412.0 4.5 %reduce_sum.28 = bf16[2,512,128]{2,1,0:T(8,128)(2,1)} reduce(f32[16,2,512,128]{3,2,1,0:T(8,128)} %bitcast.197, f32[]{:T(128)} %constant.4.clone.1), dimensions={0}, to_apply=%region_2.0 | reduce | flops 1966080 | bytes 8650756 | tf_op jit(solution)/shard_map/reduce_sum | solution.py:107
  416.6 1.7 multiply_reduce_fusion
  418.2 0.6 broadcast_multiply_fusion
  418.8 1.2 copy.114
  (28 shorter events, 0.3 us)
Async XLA Ops:
  7.2 87.3 %copy-start = (bf16[2,1024,512]{2,1,0:T(8,128)(2,1)S(1)}, bf16[2,1024,512]{2,1,0:T(8,128)(2,1)}, u32[]{:S(2)}) copy-start(bf16[2,1024,512]{2,1,0:T(8,128)(2,1)} %param.12) | copy-start | bytes 6291460
  7.2 404.8 %all-gather.3.cloned.1.call-start = ((), (), s32[]{:S(2)}) async-start(), calls=%async_computation | async-start | bytes 8912896 | tf_op jit(solution)/shard_map/all_gather | solution.py:107
  95.2 1.4 copy-start.5
  95.5 7.2 %copy-start.7 = (s32[2,2,4]{2,1,0:T(2,128)S(1)}, s32[2,2,4]{2,1,0:T(2,128)}, u32[]{:S(2)}) copy-start(s32[2,2,4]{2,1,0:T(2,128)} %param.11) | copy-start | bytes 196
  95.5 7.3 %copy-start.6 = (bf16[32,2,2,128]{3,2,1,0:T(2,128)(2,1)S(1)}, bf16[32,2,2,128]{3,2,1,0:T(2,128)(2,1)}, u32[]{:S(2)}) copy-start(bf16[32,2,2,128]{3,2,1,0:T(2,128)(2,1)} %param.13) | copy-start | bytes 98308
  97.4 27.0 %collective-permute-start.1 = (bf16[1,2,128,2,128]{4,2,1,0,3:T(8,128)(2,1)}, bf16[1,2,128,2,128]{4,2,1,0,3:T(8,128)(2,1)S(1)}, u32[]{:S(2)}, u32[]{:S(2)}) collective-permute-start(bf16[1,2,128,2,128]{4,2,1,0,3:T(8,128)(2,1)} %get-tuple-element.26), channel_id=1, source_target_pairs={{32,0},{64,32},{96,64},{128,96},{160,128},{192,160},{224,192},{256... | collective-permute-start | bytes 393224 | tf_op jit(solution)/shard_map/ppermute | solution.py:16
  99.3 25.0 %collective-permute-start = (bf16[1,2,128,2,128]{4,2,1,0,3:T(8,128)(2,1)}, bf16[1,2,128,2,128]{4,2,1,0,3:T(8,128)(2,1)S(1)}, u32[]{:S(2)}, u32[]{:S(2)}) collective-permute-start(bf16[1,2,128,2,128]{4,2,1,0,3:T(8,128)(2,1)} %get-tuple-element.27), channel_id=1, source_target_pairs={{0,32},{32,64},{64,96},{96,128},{128,160},{160,192},{192,224},{224... | collective-permute-start | bytes 393224 | tf_op jit(solution)/shard_map/ppermute | solution.py:15
  102.8 20.0 %copy-start.4 = (bf16[2,2,5,2,128,128]{5,4,3,2,1,0:T(8,128)(2,1)S(1)}, bf16[2,2,5,2,128,128]{5,4,3,2,1,0:T(8,128)(2,1)}, u32[]{:S(2)}) copy-start(bf16[2,2,5,2,128,128]{5,4,3,2,1,0:T(8,128)(2,1)} %param.10) | copy-start | bytes 3932164
  124.5 7.6 %collective-permute-start.2 = (bf16[4,1,128,2,128]{4,2,1,0,3:T(8,128)(2,1)S(1)}, bf16[4,1,128,2,128]{4,2,1,0,3:T(8,128)(2,1)S(1)}, u32[]{:S(2)}, u32[]{:S(2)}) collective-permute-start(bf16[4,1,128,2,128]{4,2,1,0,3:T(8,128)(2,1)S(1)} %get-tuple-element.22), channel_id=1, source_target_pairs={{0,1},{1,2},{2,3},{3,4},{4,5},{5,6},{6,7},{7,8},{8,9},{9,10},{10,1... | collective-permute-start | bytes 786440 | tf_op jit(solution)/shard_map/ppermute | solution.py:15
  125.8 10.5 %collective-permute-start.3 = (bf16[4,1,128,2,128]{4,2,1,0,3:T(8,128)(2,1)S(1)}, bf16[4,1,128,2,128]{4,2,1,0,3:T(8,128)(2,1)S(1)}, u32[]{:S(2)}, u32[]{:S(2)}) collective-permute-start(bf16[4,1,128,2,128]{4,2,1,0,3:T(8,128)(2,1)S(1)} %get-tuple-element.23), channel_id=1, source_target_pairs={{1,0},{2,1},{3,2},{4,3},{5,4},{6,5},{7,6},{8,7},{9,8},{10,9},{11,1... | collective-permute-start | bytes 786440 | tf_op jit(solution)/shard_map/ppermute | solution.py:16
  139.8 6.3 %copy-start.1 = (bf16[2,1024,512]{2,1,0:T(8,128)(2,1)S(1)}, bf16[2,1024,512]{2,1,0:T(8,128)(2,1)}, u32[]{:S(2)}) copy-start(bf16[2,1024,512]{2,1,0:T(8,128)(2,1)} %param.12) | copy-start | bytes 6291460
  139.9 83.8 %collective-permute-start.5 = (f32[1,2,4,128,2,128]{5,3,1,0,4,2:T(8,128)S(1)}, f32[1,2,4,128,2,128]{5,3,1,0,4,2:T(8,128)S(1)}, u32[]{:S(2)}, u32[]{:S(2)}) collective-permute-start(f32[1,2,4,128,2,128]{5,3,1,0,4,2:T(8,128)S(1)} %get-tuple-element.14), channel_id=1, source_target_pairs={{0,32},{32,64},{64,96},{96,128},{128,160},{160,192},{192,224},{224... | collective-permute-start | bytes 3145736 | tf_op jit(solution)/shard_map/ppermute | solution.py:15
  142.0 81.8 %collective-permute-start.4 = (f32[1,2,4,128,2,128]{5,3,1,0,4,2:T(8,128)S(1)}, f32[1,2,4,128,2,128]{5,3,1,0,4,2:T(8,128)S(1)}, u32[]{:S(2)}, u32[]{:S(2)}) collective-permute-start(f32[1,2,4,128,2,128]{5,3,1,0,4,2:T(8,128)S(1)} %get-tuple-element.15), channel_id=1, source_target_pairs={{32,0},{64,32},{96,64},{128,96},{160,128},{192,160},{224,192},{256... | collective-permute-start | bytes 3145736 | tf_op jit(solution)/shard_map/ppermute | solution.py:16
  223.7 1.0 copy-start.2
  223.7 1.3 copy-start.3
  227.5 189.1 %collective-permute-start.6 = (f32[4,1,4,128,2,128]{5,3,1,0,4,2:T(8,128)}, f32[4,1,4,128,2,128]{5,3,1,0,4,2:T(8,128)}, u32[]{:S(2)}, u32[]{:S(2)}) collective-permute-start(f32[4,1,4,128,2,128]{5,3,1,0,4,2:T(8,128)} %get-tuple-element.12), channel_id=1, source_target_pairs={{1,0},{2,1},{3,2},{4,3},{5,4},{6,5},{7,6},{8,7},{9,8},{10,9},{11,1... | collective-permute-start | bytes 6291464 | tf_op jit(solution)/shard_map/ppermute | solution.py:16
  228.8 187.8 %collective-permute-start.7 = (f32[4,1,4,128,2,128]{5,3,1,0,4,2:T(8,128)}, f32[4,1,4,128,2,128]{5,3,1,0,4,2:T(8,128)}, u32[]{:S(2)}, u32[]{:S(2)}) collective-permute-start(f32[4,1,4,128,2,128]{5,3,1,0,4,2:T(8,128)} %get-tuple-element.13), channel_id=1, source_target_pairs={{0,1},{1,2},{2,3},{3,4},{4,5},{5,6},{6,7},{7,8},{8,9},{9,10},{10,1... | collective-permute-start | bytes 6291464 | tf_op jit(solution)/shard_map/ppermute | solution.py:15
Sparse Core Ops, SparseCore 0:
  96.7 74.0 all-gather.2
